TPU v7x, 128 devices: a whole 4x4x4 slice. The times are simulated.
128 devices in a mesh: dp: 2 (over x_lo), phase: 16 (over z, y), tensor: 4 (over x_hi, core).
Axes of the slice: x: 4 (x_hi: 2, x_lo: 2; x = x_hi * 2 + x_lo), y: 4, z: 4, core: 2. Of those that a mesh axis runs over, the one named last changes fastest.
Arguments:
- tokens: bfloat16 [2, 2048, 8192], P('dp', 'phase', 'tensor'), may hold values from -6 to 6
- bc_proj: bfloat16 [2, 2048, 2, 2048], P('dp', 'phase', None, 'tensor'), may hold values from -0.3984375 to 0.3984375
- step_sizes: bfloat16 [2, 256, 1024], P('dp', 'phase', 'tensor'), may hold values from 0.5 to 2
- decay_rates: float32 [128], P('tensor'), may hold values from 6.1035156e-05 to 0.02
- direct_weight: float32 [128], P('tensor'), may hold values from 0.5 to 1.5
- norm_gain: float32 [8192], P('tensor'), may hold values from 0.1 to 1.9
- routes: int32 [2, 256, 1], P('dp', 'phase'), may hold values from 0 to 1; in each aligned block of 16 rows (0 to 15, 16 to 31, ..., all dimensions but the last counted through in order) at most 16 rows name the same one
- segments: int32 [2, 4096], P('dp', 'phase'), may hold values from 0 to 3, never falling along the last dimension, each value on 1 to 2048 neighbouring positions
Outputs:
- mixed: bfloat16 [2, 2048, 8192], P('dp', 'phase', 'tensor')
Inputs may be any that keep to these rules, and one draw needn't show every extreme that they name: `routes`: no device sends more than 16 of its blocks to one data group. `segments`: document ids never fall along a row; each document covers 1 to 2048 positions, and one covers exactly 2048.
All inputs are finite; a program needn't handle non-finite values.
Results may differ from a plain program's by a relative error of at most 0.0075.
Values may be sent and summed in bfloat16 or wider, within the bound.
No kernel may reach another device: no remote copies, remote signals or barrier semaphores. Data moves between devices by JAX's collectives and lax.ppermute only.
A program may use at most 128 MiB of HBM per device.

v0:
```python
import jax
import jax.numpy as jnp
from jax import lax
from jax.sharding import PartitionSpec as P

HEAD_FEATURES = 64
STATE_ENTRIES = 256
LOCAL_HEADS = 128
BLOCK = 8
EPSILON = 1e-05
PRECISE = lax.Precision.HIGHEST


def prefix(shard, axis, join, neutral):
    place = lax.axis_index(axis)
    gathered = jax.tree.map(
        lambda a, kind: lax.all_gather(a.astype(kind), axis),
        shard,
        (jnp.bfloat16, jnp.bfloat16, jnp.bfloat16, jnp.bfloat16),
    )
    state = jax.tree.map(lambda a, e: jnp.zeros_like(a) + jnp.asarray(e, a.dtype), shard, neutral)

    def one(step, state):
        return join(
            state,
            jax.tree.map(
                lambda a, own: lax.dynamic_index_in_dim(a, step, 0, False).astype(own.dtype),
                gathered,
                shard,
            ),
        )

    return lax.fori_loop(0, place, one, state)


def stretch_pass(
    carry_state, prior_id, x_stretch, b_stretch, c_stretch, dt_stretch, doc_ids, decay_rates
):
    span_len = x_stretch.shape[0]
    head_count = x_stretch.shape[1]
    groups = b_stretch.shape[1]
    per_group = head_count // groups
    log_decay = jnp.cumsum(-decay_rates[:, None] * dt_stretch, axis=1)
    x_groups = x_stretch.astype(jnp.float32).reshape(span_len, groups, per_group, -1)
    b_float = b_stretch.astype(jnp.float32)
    last_id = doc_ids[-1]
    tail_decay = (
        jnp.where(doc_ids[None, :] == last_id, jnp.exp(log_decay[:, -1:] - log_decay), 0.0)
        * dt_stretch
    )
    scaled = x_groups * tail_decay.T.reshape(span_len, groups, per_group)[..., None]
    update = jnp.einsum("jgkp,jgn->gkpn", scaled, b_float, precision=PRECISE).reshape(
        carry_state.shape
    )
    through = jnp.where(prior_id == last_id, jnp.exp(log_decay[:, -1]), 0.0)
    new_state = through[:, None, None] * carry_state + update
    positions = jnp.arange(span_len)
    same_doc = (doc_ids[:, None] == doc_ids[None, :]) & (positions[:, None] >= positions[None, :])
    gaps = jnp.minimum(log_decay[:, :, None] - log_decay[:, None, :], 0.0)
    decay_mat = jnp.where(same_doc[None], jnp.exp(gaps), 0.0) * dt_stretch[:, None, :]
    scores = jnp.einsum("ign,jgn->gij", c_stretch, b_stretch, preferred_element_type=jnp.float32)
    weights = decay_mat.reshape(groups, per_group, span_len, span_len) * scores[:, None]
    inside = jnp.einsum("gkij,jgkp->igkp", weights, x_groups, precision=PRECISE)
    state_groups = carry_state.reshape(
        groups, per_group, carry_state.shape[1], carry_state.shape[2]
    )
    carried = jnp.einsum(
        "ign,gkpn->igkp", c_stretch.astype(jnp.float32), state_groups, precision=PRECISE
    )
    keep_in = jnp.where(doc_ids[None, :] == prior_id, jnp.exp(log_decay), 0.0)
    result = inside + keep_in.T.reshape(span_len, groups, per_group)[..., None] * carried
    return (new_state, last_id, result.reshape(span_len, head_count, -1))


def local_scan(x_stretches, b_stretches, c_stretches, dt_stretches, doc_stretches, decay_rates):
    head_count = x_stretches.shape[2]

    def advance(carry, pieces):
        new_state, last_id, result = stretch_pass(
            carry[0], carry[1], pieces[0], pieces[1], pieces[2], pieces[3], pieces[4], decay_rates
        )
        return ((new_state, last_id), result)

    start_carry = (
        jnp.zeros((head_count, HEAD_FEATURES, STATE_ENTRIES), jnp.float32),
        jnp.array(-1.0, jnp.float32),
    )
    final_carry, scan_results = lax.scan(
        advance, start_carry, (x_stretches, b_stretches, c_stretches, dt_stretches, doc_stretches)
    )
    return (final_carry[0], scan_results)


def join_pieces(earlier, later):
    decay_one, state_one, first_one, last_one = earlier
    decay_two, state_two, first_two, last_two = later
    joined = (first_two == last_one) | (last_one < 0) | (first_two < 0)
    factor = jnp.where(joined, decay_two, 0.0)
    joined_state = factor[:, None, None] * state_one + state_two
    joined_decay = jnp.where(joined, decay_one * decay_two, 0.0)
    joined_first = jnp.where(first_one < 0, first_two, first_one)
    joined_last = jnp.where(last_two < 0, last_one, last_two)
    return (joined_decay, joined_state, joined_first, joined_last)


def per_device(
    tokens, bc_proj, step_sizes, decay_rates, direct_weight, norm_gain, routes, segments
):
    feature_width = tokens.shape[2]
    tok_count = tokens.shape[1]
    heads_dev = decay_rates.shape[0]
    groups_dev = bc_proj.shape[3] // STATE_ENTRIES
    per_group = heads_dev // groups_dev
    blocks = tok_count // BLOCK
    n_groups = lax.axis_size("dp")
    capacity = max(2, 2 * blocks // n_groups)
    slots = n_groups * capacity
    section = slots * BLOCK
    span_len = min(128, section)
    block_count = section // span_len
    targets = routes[0, :, 0]
    positions = jnp.arange(blocks)
    earlier = positions[:, None] > positions[None, :]
    slot_rank = jnp.sum((targets[:, None] == targets[None, :]) & earlier, axis=1)
    slot_index = targets * capacity + slot_rank
    placing = (slot_index[:, None] == jnp.arange(slots)[None, :]).astype(jnp.bfloat16)
    x_send = jnp.einsum(
        "bs,bf->sf",
        placing,
        tokens.reshape(blocks, BLOCK * feature_width),
        preferred_element_type=jnp.float32,
    )
    x_send = x_send.astype(jnp.bfloat16).reshape(n_groups, capacity, BLOCK, feature_width)
    bc_send = jnp.einsum(
        "bs,bf->sf",
        placing,
        bc_proj.reshape(blocks, BLOCK * 2 * groups_dev * STATE_ENTRIES),
        preferred_element_type=jnp.float32,
    )
    bc_send = bc_send.astype(jnp.bfloat16).reshape(
        n_groups, capacity, BLOCK, 2, groups_dev, STATE_ENTRIES
    )
    dt_send = jnp.einsum("bs,bf->sf", placing, step_sizes[0], preferred_element_type=jnp.float32)
    dt_send = dt_send.astype(jnp.bfloat16).reshape(n_groups, capacity, heads_dev * BLOCK)
    x_got, bc_got, dt_got = (
        lax.all_to_all(x_send, "dp", split_axis=0, concat_axis=0, tiled=True),
        lax.all_to_all(bc_send, "dp", split_axis=0, concat_axis=0, tiled=True),
        lax.all_to_all(dt_send, "dp", split_axis=0, concat_axis=0, tiled=True),
    )
    x_stretches = x_got.reshape(block_count, span_len, heads_dev, HEAD_FEATURES)
    b_stretches = bc_got[:, :, :, 0].reshape(block_count, span_len, groups_dev, STATE_ENTRIES)
    c_section = bc_got[:, :, :, 1].reshape(section, groups_dev, STATE_ENTRIES)
    c_stretches = c_section.reshape(block_count, span_len, groups_dev, STATE_ENTRIES)
    dt_section = (
        dt_got.reshape(slots, heads_dev, BLOCK)
        .astype(jnp.float32)
        .transpose(1, 0, 2)
        .reshape(heads_dev, section)
    )
    dt_stretches = dt_section.reshape(heads_dev, block_count, span_len).transpose(1, 0, 2)
    doc_ids = segments[0].astype(jnp.float32)
    doc_stretches = doc_ids.reshape(block_count, span_len)
    log_decay = jnp.cumsum(-decay_rates[:, None] * dt_section, axis=1)
    through = jnp.where(doc_ids[0] == doc_ids[-1], jnp.exp(log_decay[:, -1]), 0.0)
    identity = (
        jnp.ones((heads_dev,), jnp.float32),
        jnp.zeros((heads_dev, HEAD_FEATURES, STATE_ENTRIES), jnp.float32),
        jnp.array(-1.0, jnp.float32),
        jnp.array(-1.0, jnp.float32),
    )
    end_state, local_out = local_scan(
        x_stretches, b_stretches, c_stretches, dt_stretches, doc_stretches, decay_rates
    )
    incoming = prefix((through, end_state, doc_ids[0], doc_ids[-1]), "phase", join_pieces, identity)
    in_state = incoming[1]
    in_last = incoming[3]
    keep_in = jnp.where(doc_ids[None, :] == in_last, jnp.exp(log_decay), 0.0)
    state_groups = in_state.reshape(groups_dev, per_group, HEAD_FEATURES, STATE_ENTRIES)
    carried = jnp.einsum(
        "ign,gkpn->igkp", c_section.astype(jnp.float32), state_groups, precision=PRECISE
    )
    carried = carried.reshape(section, heads_dev, HEAD_FEATURES)
    combined = (
        local_out.reshape(section, heads_dev, HEAD_FEATURES) + keep_in.T[:, :, None] * carried
    )
    combined = combined + direct_weight[None, :, None] * x_got.reshape(
        section, heads_dev, HEAD_FEATURES
    ).astype(jnp.float32)
    y_section = combined.astype(jnp.bfloat16).reshape(section, feature_width)
    returned_rows = lax.all_to_all(
        y_section.reshape(n_groups, capacity, BLOCK * feature_width),
        "dp",
        split_axis=0,
        concat_axis=0,
        tiled=True,
    )
    restored = jnp.einsum(
        "bs,sf->bf",
        placing,
        returned_rows.reshape(slots, BLOCK * feature_width),
        preferred_element_type=jnp.float32,
    )
    restored = restored.astype(jnp.bfloat16).reshape(tok_count, feature_width)
    values = restored.astype(jnp.float32)
    square_sums = lax.psum(jnp.sum(values * values, axis=1), "tensor")
    mixed = (
        values
        * lax.rsqrt(square_sums / (LOCAL_HEADS * HEAD_FEATURES) + EPSILON)[:, None]
        * norm_gain
    ).astype(jnp.bfloat16)
    return mixed.reshape(1, tok_count, feature_width)


def solution(mesh):
    return jax.shard_map(
        per_device,
        mesh=mesh,
        in_specs=(
            P("dp", "phase", "tensor"),
            P("dp", "phase", None, "tensor"),
            P("dp", "phase", "tensor"),
            P("tensor"),
            P("tensor"),
            P("tensor"),
            P("dp", "phase", None),
            P("dp", "phase"),
        ),
        out_specs=P("dp", "phase", "tensor"),
        check_vma=False,
    )
```

profile of v0, /device:TPU:120, one launch (start us, length us, event | category | flops | bytes accessed | tf_op | source)
XLA Modules:
  0.0 328.3 jit_solution(4840087548735297066)
XLA Ops:
  9.0 3.2 all-to-all-start
  13.8 1.2 reshape.294
  16.1 3.5 %all-to-all-start.2 = ((bf16[2,16,8,2,2,256]{5,4,3,2,1,0:T(2,128)(2,1)}), bf16[2,16,8,2,2,256]{5,4,3,2,1,0:T(2,128)(2,1)S(1)}, u32[]{:S(2)}, u32[]{:S(2)}) async-start(bf16[2,16,8,2,2,256]{5,4,3,2,1,0:T(2,128)(2,1)} %reshape.294), calls=%async_computation.2 | async-start | bytes 1048576 | tf_op jit(solution)/shard_map/all_to_all | solution.py:147
  20.1 1.6 copy.65
  21.7 5.2 %all-to-all-done.2 = bf16[2,16,8,2,2,256]{5,4,3,2,1,0:T(2,128)(2,1)S(1)} async-done(((bf16[2,16,8,2,2,256]{5,4,3,2,1,0:T(2,128)(2,1)}), bf16[2,16,8,2,2,256]{5,4,3,2,1,0:T(2,128)(2,1)S(1)}, u32[]{:S(2)}, u32[]{:S(2)}) %all-to-all-start.2) | async-done | bytes 524320 | tf_op jit(solution)/shard_map/all_to_all | solution.py:147
  26.9 3.6 %all-to-all-start.1 = ((bf16[2,16,8,2048]{3,2,1,0:T(8,128)(2,1)}), bf16[2,16,8,2048]{3,2,1,0:T(8,128)(2,1)S(1)}, u32[]{:S(2)}, u32[]{:S(2)}) async-start(bf16[2,16,8,2048]{3,2,1,0:T(8,128)(2,1)} %bitcast.66), calls=%async_computation.1 | async-start | bytes 2097152 | tf_op jit(solution)/shard_map/all_to_all | solution.py:146
  31.6 11.0 %all-to-all-done.1 = bf16[2,16,8,2048]{3,2,1,0:T(8,128)(2,1)S(1)} async-done(((bf16[2,16,8,2048]{3,2,1,0:T(8,128)(2,1)}), bf16[2,16,8,2048]{3,2,1,0:T(8,128)(2,1)S(1)}, u32[]{:S(2)}, u32[]{:S(2)}) %all-to-all-start.1) | async-done | bytes 1048608 | tf_op jit(solution)/shard_map/all_to_all | solution.py:146
  43.7 3.2 reshape.292
  46.9 3.3 %copy.54 = bf16[2,128,32,64]{1,3,2,0:T(8,128)(2,1)S(1)} copy(bf16[2,128,32,64]{3,2,1,0:T(8,128)(2,1)} %reshape.292) | data formatting | bytes 2097152
  50.2 25.7 %while.33 = (s32[]{:T(128)}, f32[32,64,256]{2,1,0:T(8,128)}, f32[]{:T(128)}, f32[2,128,32,64]{1,3,2,0:T(8,128)}, f32[2,128]{1,0:T(2,128)S(1)}, /*index=5*/f32[32...) while((s32[]{:T(128)}, f32[32,64,256]{2,1,0:T(8,128)}, ...), condition=%wide.region_3.4_spmd.clone, body=%wide.region_1.3_spmd.clone.sunk | while | flops 2035876096 | bytes 46125748 | solution.py:88
  54.0 1.9 bitcast_add_fusion.2
  56.2 2.4 fusion.84
  60.3 1.3 copy-done.8
  66.0 3.5 %bitcast_add_fusion.2 = (f32[32,64,256]{2,1,0:T(8,128)}, f32[32,64,256]{2,1,0:T(8,128)S(1)}) fusion(f32[2,16,64,256]{3,2,1,0:T(8,128)S(1)} %fusion.81, f32[32]{0:T(128)S(1)} %broadcast_select_fusion.5, f32[32,64,256]{2,1,0:T(8,128)} %get-tuple-element.467, pred[]{:T(512)S(6)} %compare.3), kind=kLoop, calls=%fused_computation.3.clone.1 | loop fusion | flops 1572864 | bytes 8388737 | tf_op jit(solution)/shard_map/while/body/eval_jaxpr/add | solution.py:56
  69.8 2.4 fusion.84
  73.9 1.3 copy-done.8
  75.9 2.7 convert_element_type.146
  86.0 2.5 mul.184
  88.5 4.5 %mul.185 = f32[2,16,16384]{2,1,0:T(8,128)} reshape(f32[256,32,64]{2,1,0:T(8,128)} %mul.184) | data formatting | bytes 4194304 | tf_op jit(solution)/shard_map/mul | solution.py:186
  93.0 35.8 %all-reduce.3 = (bf16[16]{0:T(256)(128)(2,1)S(1)}, bf16[512]{0:T(512)(128)(2,1)S(1)}, bf16[16]{0:T(256)(128)(2,1)S(1)}) all-reduce(bf16[16]{0:T(256)(128)(2,1)S(1)} %dynamic-update-slice, bf16[512]{0:T(512)(128)(2,1)S(1)} %dynamic-update-slice.1, ...), channel_id=2, replica_groups=mesh['dp'=2,'phase'=16,'tensor'=4] {'phase'}, use_global_device_ids=true, to_apply=%add | all-reduce | flops 544 | bytes 2176 | tf_op jit(solution)/shard_map/all_gather | solution.py:17
  129.0 4.5 %copy.55 = f32[2,128,32,64]{3,2,1,0:T(8,128)} copy(f32[2,128,32,64]{1,3,2,0:T(8,128)S(1)} %copy-done.9) | data formatting | bytes 4194304 | tf_op jit(solution)/shard_map/while | solution.py:88
  133.5 4.1 %reshape.295 = f32[2,16,16384]{2,1,0:T(8,128)} reshape(f32[2,128,32,64]{3,2,1,0:T(8,128)} %copy.55) | data formatting | bytes 4194304 | tf_op jit(solution)/shard_map/reshape | solution.py:184
  137.6 1.6 reshape.304
  139.2 50.2 %all-gather.6.cloned.1.call-done = bf16[512,64,256]{2,1,0:T(8,128)(2,1)} async-done(((bf16[32,64,256]{2,1,0:T(8,128)(2,1)}), bf16[512,64,256]{2,1,0:T(8,128)(2,1)}) %all-gather.6.cloned.1.call-update) | async-done | bytes 16777232 | tf_op jit(solution)/shard_map/all_gather | solution.py:17
  189.6 82.4 %while.32 = (s32[]{:T(128)}, f32[32,64,256]{2,1,0:T(8,128)S(1)}, f32[]{:T(128)}, s32[]{:T(128)}, bf16[16]{0:T(256)(128)(2,1)S(1)}, /*index=5*/bf16[16,32]{1,0:T(...) while((s32[]{:T(128)}, f32[32,64,256]{2,1,0:T(8,128)S(1)}, ...), condition=%wide.region_7.8_spmd, body=%wide.region_6.7_spmd.sunk | while | flops 1572940 | bytes 5243423 | solution.py:33
  191.5 1.6 convert_add_fusion.2
  197.0 1.6 convert_add_fusion.2
  202.5 1.6 convert_add_fusion.2
  208.0 1.6 convert_add_fusion.2
  213.5 1.6 convert_add_fusion.2
  219.0 1.6 convert_add_fusion.2
  224.5 1.6 convert_add_fusion.2
  230.0 1.6 convert_add_fusion.2
  235.5 1.6 convert_add_fusion.2
  241.0 1.6 convert_add_fusion.2
  246.5 1.6 convert_add_fusion.2
  252.0 1.6 convert_add_fusion.2
  257.5 1.6 convert_add_fusion.2
  262.9 1.6 convert_add_fusion.2
  268.4 1.6 convert_add_fusion.2
  272.0 2.4 convolution_bitcast_fusion.1
  274.4 5.5 %copy.60 = f32[256,2,16,64]{3,2,1,0:T(8,128)} copy(f32[256,2,16,64]{0,3,2,1:T(8,128)} %convolution_bitcast_fusion.1) | data formatting | bytes 4194304 | tf_op jit(solution)/shard_map/ign,gkpn->igkp/transpose | solution.py:179
  280.0 3.9 %reshape.298 = f32[2,16,16384]{2,1,0:T(8,128)} reshape(f32[256,2,16,64]{3,2,1,0:T(8,128)} %copy.60) | data formatting | bytes 4194304 | tf_op jit(solution)/shard_map/reshape | solution.py:182
  284.0 2.6 mul.181
  286.6 4.0 %mul.182 = f32[2,16,16384]{2,1,0:T(8,128)} reshape(f32[256,32,64]{2,1,0:T(8,128)} %mul.181) | data formatting | bytes 4194304 | tf_op jit(solution)/shard_map/mul | solution.py:184
  290.6 4.2 %add_convert_fusion = bf16[2,16,16384]{2,1,0:T(8,128)(2,1)S(1)} fusion(f32[2,16,16384]{2,1,0:T(8,128)S(1)} %copy-done.6, f32[2,16,16384]{2,1,0:T(8,128)} %reshape.304, f32[2,16,16384]{2,1,0:T(8,128)} %reshape.295, f32[2,16,16384]{2,1,0:T(8,128)} %mul.182, f32[2,16,16384]{2,1,0:T(8,128)} %reshape.298), kind=kLoop, calls=%fused_computation.56 | loop fusion | flops 2621440 | bytes 11534336 | tf_op jit(solution)/shard_map/convert_element_type | solution.py:189
  294.8 16.2 %all_to_all.20 = bf16[2,16,16384]{2,1,0:T(8,128)(2,1)S(1)} all-to-all(bf16[2,16,16384]{2,1,0:T(8,128)(2,1)S(1)} %add_convert_fusion), channel_id=1, replica_groups=mesh['dp'=2,'phase'=16,'tensor'=4] {'dp'}, dimensions={0} | all-to-all | bytes 2097152 | tf_op jit(solution)/shard_map/all_to_all | solution.py:190
  311.7 8.5 %psum.7 = f32[128]{0:T(128)S(1)} all-reduce(f32[128]{0:T(128)S(1)} %reduce_sum.19), channel_id=1, replica_groups=mesh['dp'=2,'phase'=16,'tensor'=4] {'tensor'}, use_global_device_ids=true, to_apply=%region_9.10 | all-reduce | flops 128 | bytes 1024 | tf_op jit(solution)/shard_map/psum | solution.py:205
  (163 shorter events, 42.2 us)
Async XLA Ops:
  6.5 1.6 copy-start
  6.5 8.4 %copy-start.12 = (bf16[1,128,2048]{2,1,0:T(8,128)(2,1)S(1)}, bf16[1,128,2048]{2,1,0:T(8,128)(2,1)}, u32[]{:S(2)}) copy-start(bf16[1,128,2048]{2,1,0:T(8,128)(2,1)} %param.12) | copy-start | bytes 1572868
  9.0 7.1 %all-to-all-start = ((bf16[2,16,256]{2,1,0:T(8,128)(2,1)}), bf16[2,16,256]{2,1,0:T(8,128)(2,1)S(1)}, u32[]{:S(2)}, u32[]{:S(2)}) async-start(bf16[2,16,256]{2,1,0:T(8,128)(2,1)} %bitcast.9), calls=%async_computation | async-start | bytes 32768 | tf_op jit(solution)/shard_map/all_to_all | solution.py:148
  16.1 10.9 %all-to-all-start.2 = ((bf16[2,16,8,2,2,256]{5,4,3,2,1,0:T(2,128)(2,1)}), bf16[2,16,8,2,2,256]{5,4,3,2,1,0:T(2,128)(2,1)S(1)}, u32[]{:S(2)}, u32[]{:S(2)}) async-start(bf16[2,16,8,2,2,256]{5,4,3,2,1,0:T(2,128)(2,1)} %reshape.294), calls=%async_computation.2 | async-start | bytes 1048576 | tf_op jit(solution)/shard_map/all_to_all | solution.py:147
  20.1 10.5 %copy-start.16 = (f32[32]{0:T(128)S(1)}, f32[32]{0:T(128)}, u32[]{:S(2)}) copy-start(f32[32]{0:T(128)} %param.15) | copy-start | bytes 388
  20.1 10.5 %copy-start.14 = (s32[1,256]{1,0:T(1,128)S(1)}, s32[1,256]{1,0:T(1,128)}, u32[]{:S(2)}) copy-start(s32[1,256]{1,0:T(1,128)} %param.19) | copy-start | bytes 3076
  26.9 15.7 %all-to-all-start.1 = ((bf16[2,16,8,2048]{3,2,1,0:T(8,128)(2,1)}), bf16[2,16,8,2048]{3,2,1,0:T(8,128)(2,1)S(1)}, u32[]{:S(2)}, u32[]{:S(2)}) async-start(bf16[2,16,8,2048]{3,2,1,0:T(8,128)(2,1)} %bitcast.66), calls=%async_computation.1 | async-start | bytes 2097152 | tf_op jit(solution)/shard_map/all_to_all | solution.py:146
  30.5 158.8 %all-gather.6.cloned.1.call-start = ((), (), s32[]{:S(2)}) async-start(), calls=%async_computation.4 | async-start | bytes 17825792 | tf_op jit(solution)/shard_map/all_gather | solution.py:17
  31.1 15.8 %copy-start.10 = (f32[32,32,8]{0,2,1:T(8,128)}, f32[32,32,8]{0,2,1:T(8,128)S(1)}, u32[]{:S(2)}) copy-start(f32[32,32,8]{0,2,1:T(8,128)S(1)} %copy.50) | copy-start | bytes 98308
  42.7 1.1 copy-start.4
  50.2 2.1 copy-start.2
  58.6 1.6 copy-start.7
  59.7 1.9 copy-start.3
  60.3 1.3 copy-start.8
  62.3 2.1 copy-start.2
  72.2 1.6 copy-start.7
  73.4 1.9 copy-start.3
  73.9 1.3 copy-start.8
  75.9 5.8 %copy-start.17 = (u32[128]{0:T(128)S(1)}, u32[128]{0:T(128)}, u32[]{:S(2)}) copy-start(u32[128]{0:T(128)} %constant.87) | copy-start | bytes 1540
  75.9 8.6 %copy-start.11 = (f32[32,32,8]{0,2,1:T(8,128)S(1)}, f32[32,32,8]{0,2,1:T(8,128)}, u32[]{:S(2)}) copy-start(f32[32,32,8]{0,2,1:T(8,128)} %copy-done.10) | copy-start | bytes 98308
  75.9 10.0 %copy-start.15 = (f32[32]{0:T(128)S(1)}, f32[32]{0:T(128)}, u32[]{:S(2)}) copy-start(f32[32]{0:T(128)} %param.16) | copy-start | bytes 388
  88.5 40.5 %copy-start.9 = (f32[2,128,32,64]{1,3,2,0:T(8,128)S(1)}, f32[2,128,32,64]{1,3,2,0:T(8,128)}, u32[]{:S(2)}) copy-start(f32[2,128,32,64]{1,3,2,0:T(8,128)} %get-tuple-element.192) | copy-start | bytes 6291460
  133.5 4.1 %copy-start.5 = (bf16[2,16,8,2048]{3,2,1,0:T(8,128)(2,1)S(1)}, bf16[2,16,8,2048]{3,2,1,0:T(8,128)(2,1)}, u32[]{:S(2)}) copy-start(bf16[2,16,8,2048]{3,2,1,0:T(8,128)(2,1)} %copy-done.4) | copy-start | bytes 3145732
  286.6 4.0 %copy-start.6 = (f32[2,16,16384]{2,1,0:T(8,128)S(1)}, f32[2,16,16384]{2,1,0:T(8,128)}, u32[]{:S(2)}) copy-start(f32[2,16,16384]{2,1,0:T(8,128)} %mul.185) | copy-start | bytes 6291460
  311.6 8.9 %copy-start.13 = (f32[2048]{0:T(1024)S(1)}, f32[2048]{0:T(1024)}, u32[]{:S(2)}) copy-start(f32[2048]{0:T(1024)} %param.17) | copy-start | bytes 24580
  311.6 9.9 %copy-start.1 = (bf16[1,16,256]{2,1,0:T(8,128)(2,1)S(1)}, bf16[1,16,256]{2,1,0:T(8,128)(2,1)}, u32[]{:S(2)}) copy-start(bf16[1,16,256]{2,1,0:T(8,128)(2,1)} %param.14) | copy-start | bytes 24580
Sparse Core Ops, SparseCore 0:
  78.8 110.4 all-gather.5
where the time goes:
time: 330 us; the launch traced here: 328 us
  local copies, waits for them, and re-layouts  73.4 us (22%)
  waiting for transfers between devices  67.3 us (20%)
  blocking collectives  60.5 us (18%)
  other arithmetic  43.3 us (13%)
  loops' own time  42.7 us (13%)
  between operations  16.7 us (5%)
  matrix products  13.9 us (4%)
  starting transfers between devices  10.3 us (3%)
    all_gather x1, waiting for transfers between devices, prefix(): lax.all_gather(a.astype(kind), axis)  50.2 us
    another operation x1, loops' own time, prefix(): return lax.fori_loop(0, place, one, state)  39.9 us
    all_gather x1, blocking collectives, prefix(): lax.all_gather(a.astype(kind), axis)  35.8 us
    add x15, other arithmetic, join_pieces(): joined_state = factor[:, None, None] * state_one + state_two  24.7 us
    dynamic_slice x30, local copies, waits for them, and re-layouts, one(): lax.dynamic_index_in_dim(a, step, 0, False).astype(own.dtype)  17.7 us
    all_to_all x1, blocking collectives, per_device(): lax.all_to_all(y_section.reshape(n_groups, capacity, BLOCK * feature_widt...  16.2 us
    all_to_all x1, waiting for transfers between devices, per_device(): lax.all_to_all(x_send, 'dp', split_axis=0, concat_axis=0, tiled=True)  11 us
    psum x1, blocking collectives, per_device(): square_sums = lax.psum(jnp.sum(values * values, axis=1), 'tensor')  8.54 us
  transfers between devices with their start and end apart: 4, of which 4 were waited for; matrix products, arithmetic and copies ran while one was open for 8% of the time, Pallas kernels for 0%

commit v1 on v0

--- a/solution.py
+++ b/solution.py
@@ -202,7 +202,7 @@
     )
     restored = restored.astype(jnp.bfloat16).reshape(tok_count, feature_width)
     values = restored.astype(jnp.float32)
-    square_sums = lax.psum(jnp.sum(values * values, axis=1), "tensor")
+    square_sums = jnp.sum(lax.all_gather(jnp.sum(values * values, axis=1), "tensor"), axis=0)
     mixed = (
         values
         * lax.rsqrt(square_sums / (LOCAL_HEADS * HEAD_FEATURES) + EPSILON)[:, None]

time: 330 us -> 329 us (level)
    psum x1 -> x0, blocking collectives: 8.54 us -> none  [per_device(): square_sums = lax.psum(jnp.sum(values * values, axis=1), 'tensor')]
    all_gather x0 -> x1, blocking collectives: none -> 6.56 us  [per_device(): lax.all_gather(jnp.sum(values * values, axis=1), 'tensor')]
where the time goes in v1:
time: 329 us; the launch traced here: 326 us
  local copies, waits for them, and re-layouts  73.4 us (22%)
  waiting for transfers between devices  67.3 us (20%)
  blocking collectives  58.6 us (18%)
  other arithmetic  43.3 us (13%)
  loops' own time  42.7 us (13%)
  between operations  16.7 us (5%)
  matrix products  13.9 us (4%)
  starting transfers between devices  10.3 us (3%)
    all_gather x1, waiting for transfers between devices, prefix(): lax.all_gather(a.astype(kind), axis)  50.2 us
    another operation x1, loops' own time, prefix(): return lax.fori_loop(0, place, one, state)  39.9 us
    all_gather x1, blocking collectives, prefix(): lax.all_gather(a.astype(kind), axis)  35.8 us
    add x15, other arithmetic, join_pieces(): joined_state = factor[:, None, None] * state_one + state_two  24.7 us
    dynamic_slice x30, local copies, waits for them, and re-layouts, one(): lax.dynamic_index_in_dim(a, step, 0, False).astype(own.dtype)  17.7 us
    all_to_all x1, blocking collectives, per_device(): lax.all_to_all(y_section.reshape(n_groups, capacity, BLOCK * feature_widt...  16.2 us
    all_to_all x1, waiting for transfers between devices, per_device(): lax.all_to_all(x_send, 'dp', split_axis=0, concat_axis=0, tiled=True)  11 us
    unnamed x38, local copies, waits for them, and re-layouts  8.53 us
  transfers between devices with their start and end apart: 4, of which 4 were waited for; matrix products, arithmetic and copies ran while one was open for 8% of the time, Pallas kernels for 0%

profile of v1, /device:TPU:120, one launch (start us, length us, event | category | flops | bytes accessed | tf_op | source)
XLA Modules:
  0.0 326.3 jit_solution(1781413549889477510)
XLA Ops:
  9.0 3.2 all-to-all-start
  13.8 1.2 reshape.300
  16.1 3.5 %all-to-all-start.2 = ((bf16[2,16,8,2,2,256]{5,4,3,2,1,0:T(2,128)(2,1)}), bf16[2,16,8,2,2,256]{5,4,3,2,1,0:T(2,128)(2,1)S(1)}, u32[]{:S(2)}, u32[]{:S(2)}) async-start(bf16[2,16,8,2,2,256]{5,4,3,2,1,0:T(2,128)(2,1)} %reshape.300), calls=%async_computation.2 | async-start | bytes 1048576 | tf_op jit(solution)/shard_map/all_to_all | solution.py:147
  20.1 1.6 copy.65
  21.7 5.2 %all-to-all-done.2 = bf16[2,16,8,2,2,256]{5,4,3,2,1,0:T(2,128)(2,1)S(1)} async-done(((bf16[2,16,8,2,2,256]{5,4,3,2,1,0:T(2,128)(2,1)}), bf16[2,16,8,2,2,256]{5,4,3,2,1,0:T(2,128)(2,1)S(1)}, u32[]{:S(2)}, u32[]{:S(2)}) %all-to-all-start.2) | async-done | bytes 524320 | tf_op jit(solution)/shard_map/all_to_all | solution.py:147
  26.9 3.6 %all-to-all-start.1 = ((bf16[2,16,8,2048]{3,2,1,0:T(8,128)(2,1)}), bf16[2,16,8,2048]{3,2,1,0:T(8,128)(2,1)S(1)}, u32[]{:S(2)}, u32[]{:S(2)}) async-start(bf16[2,16,8,2048]{3,2,1,0:T(8,128)(2,1)} %bitcast.67), calls=%async_computation.1 | async-start | bytes 2097152 | tf_op jit(solution)/shard_map/all_to_all | solution.py:146
  31.6 11.0 %all-to-all-done.1 = bf16[2,16,8,2048]{3,2,1,0:T(8,128)(2,1)S(1)} async-done(((bf16[2,16,8,2048]{3,2,1,0:T(8,128)(2,1)}), bf16[2,16,8,2048]{3,2,1,0:T(8,128)(2,1)S(1)}, u32[]{:S(2)}, u32[]{:S(2)}) %all-to-all-start.1) | async-done | bytes 1048608 | tf_op jit(solution)/shard_map/all_to_all | solution.py:146
  43.7 3.2 reshape.298
  46.9 3.3 %copy.54 = bf16[2,128,32,64]{1,3,2,0:T(8,128)(2,1)S(1)} copy(bf16[2,128,32,64]{3,2,1,0:T(8,128)(2,1)} %reshape.298) | data formatting | bytes 2097152
  50.2 25.7 %while.33 = (s32[]{:T(128)}, f32[32,64,256]{2,1,0:T(8,128)}, f32[]{:T(128)}, f32[2,128,32,64]{1,3,2,0:T(8,128)}, f32[2,128]{1,0:T(2,128)S(1)}, /*index=5*/f32[32...) while((s32[]{:T(128)}, f32[32,64,256]{2,1,0:T(8,128)}, ...), condition=%wide.region_3.4_spmd.clone, body=%wide.region_1.3_spmd.clone.sunk | while | flops 2035876096 | bytes 46125748 | solution.py:88
  54.0 1.9 bitcast_add_fusion.2
  56.2 2.4 fusion.84
  60.3 1.3 copy-done.8
  66.0 3.5 %bitcast_add_fusion.2 = (f32[32,64,256]{2,1,0:T(8,128)}, f32[32,64,256]{2,1,0:T(8,128)S(1)}) fusion(f32[2,16,64,256]{3,2,1,0:T(8,128)S(1)} %fusion.81, f32[32]{0:T(128)S(1)} %broadcast_select_fusion.5, f32[32,64,256]{2,1,0:T(8,128)} %get-tuple-element.467, pred[]{:T(512)S(6)} %compare.3), kind=kLoop, calls=%fused_computation.3.clone.1 | loop fusion | flops 1572864 | bytes 8388737 | tf_op jit(solution)/shard_map/while/body/eval_jaxpr/add | solution.py:56
  69.8 2.4 fusion.84
  73.9 1.3 copy-done.8
  75.9 2.7 convert_element_type.146
  86.0 2.5 mul.184
  88.5 4.5 %mul.185 = f32[2,16,16384]{2,1,0:T(8,128)} reshape(f32[256,32,64]{2,1,0:T(8,128)} %mul.184) | data formatting | bytes 4194304 | tf_op jit(solution)/shard_map/mul | solution.py:186
  93.0 35.8 %all-reduce.3 = (bf16[16]{0:T(256)(128)(2,1)S(1)}, bf16[512]{0:T(512)(128)(2,1)S(1)}, bf16[16]{0:T(256)(128)(2,1)S(1)}) all-reduce(bf16[16]{0:T(256)(128)(2,1)S(1)} %dynamic-update-slice, bf16[512]{0:T(512)(128)(2,1)S(1)} %dynamic-update-slice.1, ...), channel_id=2, replica_groups=mesh['dp'=2,'phase'=16,'tensor'=4] {'phase'}, use_global_device_ids=true, to_apply=%add | all-reduce | flops 544 | bytes 2176 | tf_op jit(solution)/shard_map/all_gather | solution.py:17
  129.0 4.5 %copy.55 = f32[2,128,32,64]{3,2,1,0:T(8,128)} copy(f32[2,128,32,64]{1,3,2,0:T(8,128)S(1)} %copy-done.9) | data formatting | bytes 4194304 | tf_op jit(solution)/shard_map/while | solution.py:88
  133.5 4.1 %reshape.301 = f32[2,16,16384]{2,1,0:T(8,128)} reshape(f32[2,128,32,64]{3,2,1,0:T(8,128)} %copy.55) | data formatting | bytes 4194304 | tf_op jit(solution)/shard_map/reshape | solution.py:184
  137.6 1.6 reshape.310
  139.2 50.2 %all-gather.8.cloned.1.call-done = bf16[512,64,256]{2,1,0:T(8,128)(2,1)} async-done(((bf16[32,64,256]{2,1,0:T(8,128)(2,1)}), bf16[512,64,256]{2,1,0:T(8,128)(2,1)}) %all-gather.8.cloned.1.call-update) | async-done | bytes 16777232 | tf_op jit(solution)/shard_map/all_gather | solution.py:17
  189.6 82.4 %while.32 = (s32[]{:T(128)}, f32[32,64,256]{2,1,0:T(8,128)S(1)}, f32[]{:T(128)}, s32[]{:T(128)}, bf16[16]{0:T(256)(128)(2,1)S(1)}, /*index=5*/bf16[16,32]{1,0:T(...) while((s32[]{:T(128)}, f32[32,64,256]{2,1,0:T(8,128)S(1)}, ...), condition=%wide.region_7.8_spmd, body=%wide.region_6.7_spmd.sunk | while | flops 1572940 | bytes 5243423 | solution.py:33
  191.5 1.6 convert_add_fusion.2
  197.0 1.6 convert_add_fusion.2
  202.5 1.6 convert_add_fusion.2
  208.0 1.6 convert_add_fusion.2
  213.5 1.6 convert_add_fusion.2
  219.0 1.6 convert_add_fusion.2
  224.5 1.6 convert_add_fusion.2
  230.0 1.6 convert_add_fusion.2
  235.5 1.6 convert_add_fusion.2
  241.0 1.6 convert_add_fusion.2
  246.5 1.6 convert_add_fusion.2
  252.0 1.6 convert_add_fusion.2
  257.5 1.6 convert_add_fusion.2
  262.9 1.6 convert_add_fusion.2
  268.4 1.6 convert_add_fusion.2
  272.0 2.4 convolution_bitcast_fusion.1
  274.4 5.5 %copy.60 = f32[256,2,16,64]{3,2,1,0:T(8,128)} copy(f32[256,2,16,64]{0,3,2,1:T(8,128)} %convolution_bitcast_fusion.1) | data formatting | bytes 4194304 | tf_op jit(solution)/shard_map/ign,gkpn->igkp/transpose | solution.py:179
  280.0 3.9 %reshape.304 = f32[2,16,16384]{2,1,0:T(8,128)} reshape(f32[256,2,16,64]{3,2,1,0:T(8,128)} %copy.60) | data formatting | bytes 4194304 | tf_op jit(solution)/shard_map/reshape | solution.py:182
  284.0 2.6 mul.181
  286.6 4.0 %mul.182 = f32[2,16,16384]{2,1,0:T(8,128)} reshape(f32[256,32,64]{2,1,0:T(8,128)} %mul.181) | data formatting | bytes 4194304 | tf_op jit(solution)/shard_map/mul | solution.py:184
  290.6 4.2 %add_convert_fusion = bf16[2,16,16384]{2,1,0:T(8,128)(2,1)S(1)} fusion(f32[2,16,16384]{2,1,0:T(8,128)S(1)} %copy-done.6, f32[2,16,16384]{2,1,0:T(8,128)} %reshape.310, f32[2,16,16384]{2,1,0:T(8,128)} %reshape.301, f32[2,16,16384]{2,1,0:T(8,128)} %mul.182, f32[2,16,16384]{2,1,0:T(8,128)} %reshape.304), kind=kLoop, calls=%fused_computation.56 | loop fusion | flops 2621440 | bytes 11534336 | tf_op jit(solution)/shard_map/convert_element_type | solution.py:189
  294.8 16.2 %all_to_all.20 = bf16[2,16,16384]{2,1,0:T(8,128)(2,1)S(1)} all-to-all(bf16[2,16,16384]{2,1,0:T(8,128)(2,1)S(1)} %add_convert_fusion), channel_id=1, replica_groups=mesh['dp'=2,'phase'=16,'tensor'=4] {'dp'}, dimensions={0} | all-to-all | bytes 2097152 | tf_op jit(solution)/shard_map/all_to_all | solution.py:190
  311.7 6.6 %all-gather.5 = f32[4,1,128]{2,1,0:T(1,128)S(1)} all-gather(f32[1,1,128]{2,1,0:T(1,128)S(1)} %bitcast.193), channel_id=6, replica_groups=mesh['dp'=2,'phase'=16,'tensor'=4] {'tensor'}, dimensions={0}, use_global_device_ids=true | all-gather | bytes 2560 | tf_op jit(solution)/shard_map/all_gather | solution.py:205
  (164 shorter events, 42.2 us)
Async XLA Ops:
  6.5 1.6 copy-start
  6.5 8.4 %copy-start.12 = (bf16[1,128,2048]{2,1,0:T(8,128)(2,1)S(1)}, bf16[1,128,2048]{2,1,0:T(8,128)(2,1)}, u32[]{:S(2)}) copy-start(bf16[1,128,2048]{2,1,0:T(8,128)(2,1)} %param.12) | copy-start | bytes 1572868
  9.0 7.1 %all-to-all-start = ((bf16[2,16,256]{2,1,0:T(8,128)(2,1)}), bf16[2,16,256]{2,1,0:T(8,128)(2,1)S(1)}, u32[]{:S(2)}, u32[]{:S(2)}) async-start(bf16[2,16,256]{2,1,0:T(8,128)(2,1)} %bitcast.9), calls=%async_computation | async-start | bytes 32768 | tf_op jit(solution)/shard_map/all_to_all | solution.py:148
  16.1 10.9 %all-to-all-start.2 = ((bf16[2,16,8,2,2,256]{5,4,3,2,1,0:T(2,128)(2,1)}), bf16[2,16,8,2,2,256]{5,4,3,2,1,0:T(2,128)(2,1)S(1)}, u32[]{:S(2)}, u32[]{:S(2)}) async-start(bf16[2,16,8,2,2,256]{5,4,3,2,1,0:T(2,128)(2,1)} %reshape.300), calls=%async_computation.2 | async-start | bytes 1048576 | tf_op jit(solution)/shard_map/all_to_all | solution.py:147
  20.1 10.5 %copy-start.16 = (f32[32]{0:T(128)S(1)}, f32[32]{0:T(128)}, u32[]{:S(2)}) copy-start(f32[32]{0:T(128)} %param.15) | copy-start | bytes 388
  20.1 10.5 %copy-start.14 = (s32[1,256]{1,0:T(1,128)S(1)}, s32[1,256]{1,0:T(1,128)}, u32[]{:S(2)}) copy-start(s32[1,256]{1,0:T(1,128)} %param.19) | copy-start | bytes 3076
  26.9 15.7 %all-to-all-start.1 = ((bf16[2,16,8,2048]{3,2,1,0:T(8,128)(2,1)}), bf16[2,16,8,2048]{3,2,1,0:T(8,128)(2,1)S(1)}, u32[]{:S(2)}, u32[]{:S(2)}) async-start(bf16[2,16,8,2048]{3,2,1,0:T(8,128)(2,1)} %bitcast.67), calls=%async_computation.1 | async-start | bytes 2097152 | tf_op jit(solution)/shard_map/all_to_all | solution.py:146
  30.5 158.8 %all-gather.8.cloned.1.call-start = ((), (), s32[]{:S(2)}) async-start(), calls=%async_computation.4 | async-start | bytes 17825792 | tf_op jit(solution)/shard_map/all_gather | solution.py:17
  31.1 15.8 %copy-start.10 = (f32[32,32,8]{0,2,1:T(8,128)}, f32[32,32,8]{0,2,1:T(8,128)S(1)}, u32[]{:S(2)}) copy-start(f32[32,32,8]{0,2,1:T(8,128)S(1)} %copy.50) | copy-start | bytes 98308
  42.7 1.1 copy-start.4
  50.2 2.1 copy-start.2
  58.6 1.6 copy-start.7
  59.7 1.9 copy-start.3
  60.3 1.3 copy-start.8
  62.3 2.1 copy-start.2
  72.2 1.6 copy-start.7
  73.4 1.9 copy-start.3
  73.9 1.3 copy-start.8
  75.9 5.8 %copy-start.17 = (u32[128]{0:T(128)S(1)}, u32[128]{0:T(128)}, u32[]{:S(2)}) copy-start(u32[128]{0:T(128)} %constant.87) | copy-start | bytes 1540
  75.9 8.6 %copy-start.11 = (f32[32,32,8]{0,2,1:T(8,128)S(1)}, f32[32,32,8]{0,2,1:T(8,128)}, u32[]{:S(2)}) copy-start(f32[32,32,8]{0,2,1:T(8,128)} %copy-done.10) | copy-start | bytes 98308
  75.9 10.0 %copy-start.15 = (f32[32]{0:T(128)S(1)}, f32[32]{0:T(128)}, u32[]{:S(2)}) copy-start(f32[32]{0:T(128)} %param.16) | copy-start | bytes 388
  88.5 40.5 %copy-start.9 = (f32[2,128,32,64]{1,3,2,0:T(8,128)S(1)}, f32[2,128,32,64]{1,3,2,0:T(8,128)}, u32[]{:S(2)}) copy-start(f32[2,128,32,64]{1,3,2,0:T(8,128)} %get-tuple-element.192) | copy-start | bytes 6291460
  133.5 4.1 %copy-start.5 = (bf16[2,16,8,2048]{3,2,1,0:T(8,128)(2,1)S(1)}, bf16[2,16,8,2048]{3,2,1,0:T(8,128)(2,1)}, u32[]{:S(2)}) copy-start(bf16[2,16,8,2048]{3,2,1,0:T(8,128)(2,1)} %copy-done.4) | copy-start | bytes 3145732
  286.6 4.0 %copy-start.6 = (f32[2,16,16384]{2,1,0:T(8,128)S(1)}, f32[2,16,16384]{2,1,0:T(8,128)}, u32[]{:S(2)}) copy-start(f32[2,16,16384]{2,1,0:T(8,128)} %mul.185) | copy-start | bytes 6291460
  311.6 7.0 %copy-start.13 = (f32[2048]{0:T(1024)S(1)}, f32[2048]{0:T(1024)}, u32[]{:S(2)}) copy-start(f32[2048]{0:T(1024)} %param.17) | copy-start | bytes 24580
  311.6 7.9 %copy-start.1 = (bf16[1,16,256]{2,1,0:T(8,128)(2,1)S(1)}, bf16[1,16,256]{2,1,0:T(8,128)(2,1)}, u32[]{:S(2)}) copy-start(bf16[1,16,256]{2,1,0:T(8,128)(2,1)} %param.14) | copy-start | bytes 24580
Sparse Core Ops, SparseCore 0:
  78.8 110.4 all-gather.7
